TPU v7x, 32 devices: a whole 2x2x4 slice. The times are simulated.
32 devices in a mesh: expert: 8 (over z, y), blk: 4 (over x, core).
Axes of the slice: x: 2, y: 2, z: 4, core: 2. Of those that a mesh axis runs over, the one named last changes fastest.
Arguments:
- inputs: bfloat16 [8, 768, 1536], P('expert', 'blk'), may hold values from -6 to 6
- output_grads: bfloat16 [8, 768, 4096], P('expert', 'blk'), may hold values from -0.21875 to 0.21875
- route_counts: int32 [8, 4], P('expert', 'blk'), may hold values from 48 to 192, as said below
- left_rows: bfloat16 [8, 2304, 1536], P(None, 'expert', 'blk'), as said below
- left_lengths: int32 [8, 8], replicated, may hold values from 96 to 288, as said below
- right_inverse: bfloat16 [8, 4096, 4096], P('expert', 'blk'), may hold values from -0.09375 to 0.09375
Outputs:
- preconditioned: float32 [8, 4096, 1536], P('expert', 'blk')
Inputs may be any that keep to these rules, and one draw needn't show every extreme that they name: `route_counts`: for every expert, one device of blk holds exactly 192 routed tokens and one holds exactly 48. `left_lengths`: each row sums to 1536; in each row one owner holds exactly 288 rows and one exactly 96. `left_rows`: slots i * 288 + j with j >= left_lengths[e, i] are zero.
All inputs are finite; a program needn't handle non-finite values.
Results may differ from a plain program's by a relative error of at most 0.0041.
Values may be sent and summed in bfloat16 or wider, within the bound.
A program may use at most 128 MiB of HBM per device.

v0:
```python
import jax
import jax.numpy as jnp
from jax import lax
from jax.sharding import PartitionSpec as P


def shards(inputs, output_grads, route_counts, left_rows, left_lengths, right_inverse):
    token_rows = inputs[0]
    grad_rows = output_grads[0]
    slot_count = token_rows.shape[0]
    width_in = token_rows.shape[1]
    live_rows = lax.broadcasted_iota(jnp.int32, (slot_count, 1), 0) < route_counts[0, 0]
    masked = jnp.where(live_rows, token_rows, jnp.zeros_like(token_rows))
    contract_rows = (((0,), (0,)), ((), ()))
    columns = lax.all_to_all(grad_rows, "blk", split_axis=1, concat_axis=0, tiled=True)
    gradient = lax.dot_general(
        columns,
        lax.all_gather(masked, "blk", axis=0, tiled=True),
        contract_rows,
        preferred_element_type=jnp.float32,
    )
    gradient = gradient.astype(jnp.bfloat16)
    own_expert = lax.axis_index("expert")
    lengths = lax.dynamic_index_in_dim(left_lengths, own_expert, 0, keepdims=False)
    starts = jnp.cumsum(lengths) - lengths
    owners = lengths.shape[0]
    piece_slots = left_rows.shape[1]
    offset = lax.broadcasted_iota(jnp.int32, (owners, piece_slots), 1)
    row_index = jnp.minimum(starts[:, None] + offset, width_in - 1).reshape(owners * piece_slots)
    kept_rows = (offset < lengths[:, None]).reshape(1, owners * piece_slots)
    picked = jnp.where(
        kept_rows, jnp.take(gradient, row_index, axis=1), jnp.zeros((), jnp.bfloat16)
    )
    arrived = lax.all_to_all(left_rows, "expert", split_axis=0, concat_axis=1, tiled=True)
    weighted = jnp.dot(
        picked,
        lax.all_gather(arrived, "blk", axis=2, tiled=True)[0],
        preferred_element_type=jnp.float32,
    ).astype(jnp.bfloat16)
    inverse_rows = right_inverse[0]
    everything = lax.all_gather(weighted, "blk", axis=0, tiled=True)
    result = jnp.dot(inverse_rows, everything, preferred_element_type=jnp.float32)
    return result[None]


def solution(mesh):
    in_specs = (
        P("expert", "blk", None),
        P("expert", "blk", None),
        P("expert", "blk"),
        P(None, "expert", "blk"),
        P(),
        P("expert", "blk", None),
    )
    out_specs = P("expert", "blk", None)
    return jax.shard_map(shards, mesh=mesh, in_specs=in_specs, out_specs=out_specs, check_vma=False)
```

profile of v0, /device:TPU:0, one launch (start us, length us, event | category | flops | bytes accessed | tf_op | source)
XLA Modules:
  0.0 251.2 jit_solution(289022120514469136)
XLA Ops:
  6.5 0.0 copy-start
  6.5 0.0 all-gather.4.cloned.1.call-start
  7.3 2.0 bitcast_select_fusion
  9.3 0.0 all-gather.4.cloned.1.call-update
  9.3 0.0 all-gather.6.cloned.1.call-start
  9.4 48.7 %all_to_all.31 = bf16[8,288,384]{2,1,0:T(8,128)(2,1)} all-to-all(bf16[8,288,384]{2,1,0:T(8,128)(2,1)} %param.9), channel_id=1, replica_groups=mesh['expert'=8,'blk'=4] {'expert'}, dimensions={0} | all-to-all | bytes 3538944 | tf_op jit(solution)/shard_map/all_to_all | solution.py:34
  58.1 0.0 all-gather.6.cloned.1.call-update
  58.1 0.0 copy-done
  58.1 1.2 all_to_all.23
  59.3 1.6 copy.11
  60.9 3.6 %all-to-all-start = ((bf16[192,4,1024]{2,0,1:T(8,128)(2,1)}), bf16[192,4,1024]{2,0,1:T(8,128)(2,1)S(1)}, u32[]{:S(2)}, u32[]{:S(2)}) async-start(bf16[192,4,1024]{2,0,1:T(8,128)(2,1)} %copy.11), calls=%async_computation | async-start | bytes 3145728 | tf_op jit(solution)/shard_map/all_to_all | solution.py:15
  64.5 0.0 all-gather.8.cloned.1.call-start
  64.6 0.7 fusion.20
  65.3 0.2 reduce-window.8
  65.5 0.7 bitcast_subtract_fusion
  66.2 0.1 add_minimum_fusion
  66.3 0.1 min.28
  66.3 0.1 min.26
  66.4 0.1 iota_compare_fusion
  66.5 0.1 lt.57
  66.7 34.6 %all-to-all-done = bf16[192,4,1024]{2,0,1:T(8,128)(2,1)S(1)} async-done(((bf16[192,4,1024]{2,0,1:T(8,128)(2,1)}), bf16[192,4,1024]{2,0,1:T(8,128)(2,1)S(1)}, u32[]{:S(2)}, u32[]{:S(2)}) %all-to-all-start) | async-done | bytes 1572896 | tf_op jit(solution)/shard_map/all_to_all | solution.py:15
  101.2 0.0 copy-start.1
  101.2 0.0 all-gather.4.cloned.1.call-done
  101.2 1.1 copy-done.1
  102.4 4.8 %fusion.16 = bf16[1024,1536]{0,1:T(8,128)(2,1)S(1)} fusion(bf16[768,1536]{1,0:T(8,128)(2,1)} %all-gather.4.cloned.1.call-done, bf16[768,1024]{1,0:T(8,128)(2,1)} %bitcast.35), kind=kOutput, calls=%fused_computation.12 | convolution fusion | flops 2417491968 | bytes 7077888 | tf_op jit(solution)/shard_map/dot_general | solution.py:16
  107.1 8.1 %gather_fusion = bf16[2304,1024]{1,0:T(8,128)(2,1)} fusion(bf16[1024,1536]{0,1:T(8,128)(2,1)S(1)} %fusion.16, s32[3072]{0:T(1024)S(1)} %pad_clamp_fusion), kind=kCustom, calls=%fused_computation | custom fusion | bytes 9446400 | tf_op jit(solution)/shard_map/jit(_take)/gather | solution.py:32
  115.2 8.9 %all-gather.6.cloned.1.call-done = bf16[1,2304,1536]{2,1,0:T(8,128)(2,1)} async-done(((bf16[1,2304,384]{2,1,0:T(8,128)(2,1)}), bf16[1,2304,1536]{2,1,0:T(8,128)(2,1)}) %all-gather.6.cloned.1.call-update) | async-done | bytes 7077904 | tf_op jit(solution)/shard_map/all_gather | solution.py:37
  124.1 14.1 %fusion.11 = bf16[1024,1536]{1,0:T(8,128)(2,1)} fusion(bf16[1,2304,1536]{2,1,0:T(8,128)(2,1)} %all-gather.6.cloned.1.call-done, bf16[2304,1024]{1,0:T(8,128)(2,1)} %gather_fusion, pred[2304]{0:T(1024)(128)(4,1)S(1)} %lt.57, pred[2304]{0:T(1024)(128)(4,1)S(1)} %compare_and_fusion), kind=kOutput, calls=%fused_computation.10 | convolution fusion | flops 7254048768 | bytes 14946816 | tf_op jit(solution)/shard_map/dot_general | solution.py:35
  138.2 0.0 all-gather.8.cloned.1.call-update
  138.3 80.2 %all-gather.8.cloned.1.call-done = bf16[4096,1536]{1,0:T(8,128)(2,1)} async-done(((bf16[1024,1536]{1,0:T(8,128)(2,1)}), bf16[4096,1536]{1,0:T(8,128)(2,1)}) %all-gather.8.cloned.1.call-update) | async-done | bytes 12582928 | tf_op jit(solution)/shard_map/all_gather | solution.py:41
  218.5 19.7 %fusion.8 = f32[1,1024,1536]{1,2,0:T(8,128)} fusion(bf16[4096,1536]{1,0:T(8,128)(2,1)} %all-gather.8.cloned.1.call-done, bf16[1,1024,4096]{2,1,0:T(8,128)(2,1)} %param.11), kind=kOutput, calls=%fused_computation.9 | convolution fusion | flops 12884901888 | bytes 27262976 | tf_op jit(solution)/shard_map/dot_general | solution.py:42
  238.2 6.6 %copy.12 = f32[1,1024,1536]{2,1,0:T(8,128)} copy(f32[1,1024,1536]{1,2,0:T(8,128)} %fusion.8) | data formatting | bytes 12582912 | tf_op jit(solution)/shard_map/broadcast_in_dim | solution.py:43
  (4 shorter events, 0.1 us)
Async XLA Ops:
  6.5 51.6 %copy-start = (bf16[1,192,4096]{2,1,0:T(8,128)(2,1)S(1)}, bf16[1,192,4096]{2,1,0:T(8,128)(2,1)}, u32[]{:S(2)}) copy-start(bf16[1,192,4096]{2,1,0:T(8,128)(2,1)} %param.7) | copy-start | bytes 4718596
  6.5 94.7 %all-gather.4.cloned.1.call-start = ((), (), s32[]{:S(2)}) async-start(), calls=%async_computation.2 | async-start | bytes 2949120 | tf_op jit(solution)/shard_map/all_gather | solution.py:18
  9.3 114.8 %all-gather.6.cloned.1.call-start = ((), (), s32[]{:S(2)}) async-start(), calls=%async_computation.3 | async-start | bytes 8847360 | tf_op jit(solution)/shard_map/all_gather | solution.py:37
  60.9 40.3 %all-to-all-start = ((bf16[192,4,1024]{2,0,1:T(8,128)(2,1)}), bf16[192,4,1024]{2,0,1:T(8,128)(2,1)S(1)}, u32[]{:S(2)}, u32[]{:S(2)}) async-start(bf16[192,4,1024]{2,0,1:T(8,128)(2,1)} %copy.11), calls=%async_computation | async-start | bytes 3145728 | tf_op jit(solution)/shard_map/all_to_all | solution.py:15
  64.5 153.9 %all-gather.8.cloned.1.call-start = ((), (), s32[]{:S(2)}) async-start(), calls=%async_computation.4 | async-start | bytes 15728640 | tf_op jit(solution)/shard_map/all_gather | solution.py:41
  101.2 1.1 copy-start.1
Sparse Core Ops, SparseCore 0:
  9.5 26.7 all-gather.3
  58.2 65.8 all-gather.5
  138.4 80.0 all-gather.7
where the time goes:
time: 252 us; the launch traced here: 251 us
  waiting for transfers between devices  124 us (49%)
  blocking collectives  48.7 us (19%)
  matrix products  38.6 us (15%)
  local copies, waits for them, and re-layouts  19.5 us (8%)
  between operations  13.9 us (6%)
  starting transfers between devices  3.7 us (1%)
  other arithmetic  3.08 us (1%)
    all_gather x1, waiting for transfers between devices, shards(): everything = lax.all_gather(weighted, 'blk', axis=0, tiled=True)  80.2 us
    all_to_all x1, blocking collectives, shards(): lax.all_to_all(left_rows, 'expert', split_axis=0, concat_axis=1, tiled=True)  48.7 us
    all_to_all x1, waiting for transfers between devices, shards(): lax.all_to_all(grad_rows, 'blk', split_axis=1, concat_axis=0, tiled=True)  34.6 us
    dot_general x1, matrix products, shards(): jnp.dot(inverse_rows, everything, preferred_element_type=jnp.float32)  19.7 us
    dot_general x1, matrix products, shards(): jnp.dot(picked, lax.all_gather(arrived, 'blk', axis=2, tiled=True)[0], pr...  14.1 us
    all_gather x1, waiting for transfers between devices, shards(): lax.all_gather(arrived, 'blk', axis=2, tiled=True)[0]  8.9 us
    gather x1, local copies, waits for them, and re-layouts, shards(): jnp.take(gradient, row_index, axis=1)  8.06 us
    broadcast_in_dim x1, local copies, waits for them, and re-layouts, shards(): return result[None]  6.56 us
  transfers between devices with their start and end apart: 4, of which 3 were waited for; matrix products, arithmetic and copies ran while one was open for 7% of the time, Pallas kernels for 0%

commit v1 on v0

--- a/solution.py
+++ b/solution.py
@@ -12,7 +12,19 @@
     live_rows = lax.broadcasted_iota(jnp.int32, (slot_count, 1), 0) < route_counts[0, 0]
     masked = jnp.where(live_rows, token_rows, jnp.zeros_like(token_rows))
     contract_rows = (((0,), (0,)), ((), ()))
-    columns = lax.all_to_all(grad_rows, "blk", split_axis=1, concat_axis=0, tiled=True)
+    ways, here = (lax.axis_size("blk"), lax.axis_index("blk"))
+    width = grad_rows.shape[1] // ways
+    shape = list(grad_rows.shape)
+    shape[1] = width
+    height = shape[0]
+    shape[0] = height * ways
+    full = jnp.zeros(shape, grad_rows.dtype)
+    for mask in range(ways):
+        part = lax.dynamic_slice_in_dim(grad_rows, (here ^ mask) * width, width, axis=1)
+        if mask:
+            part = lax.ppermute(part, "blk", [(d, d ^ mask) for d in range(ways)])
+        full = lax.dynamic_update_slice_in_dim(full, part, (here ^ mask) * height, axis=0)
+    columns = full
     gradient = lax.dot_general(
         columns,
         lax.all_gather(masked, "blk", axis=0, tiled=True),

time: 252 us -> 246 us (0.976)
  waiting for transfers between devices: 124 us -> 113 us
  local copies, waits for them, and re-layouts: 19.5 us -> 22.9 us
  other arithmetic: 3.08 us -> 6.13 us
    all_to_all x1 -> x0, waiting for transfers between devices: 34.6 us -> none  [shards(): lax.all_to_all(grad_rows, 'blk', split_axis=1, concat_axis=0, tiled=True)]
    ppermute x0 -> x3, waiting for transfers between devices: none -> 16.7 us  [shards(): part = lax.ppermute(part, 'blk', [(d, d ^ mask) for d in range(ways)])]
    all_gather x1, waiting for transfers between devices: 8.9 us -> 15.3 us  [shards(): lax.all_gather(arrived, 'blk', axis=2, tiled=True)[0]]
    dynamic_update_slice x0 -> x4, local copies, waits for them, and re-layouts: none -> 4.1 us  [shards(): lax.dynamic_update_slice_in_dim(full, part, (here ^ mask) * height, axis=0)]
    all_to_all x1 -> x0, starting transfers between devices: 3.61 us -> none  [shards(): lax.all_to_all(grad_rows, 'blk', split_axis=1, concat_axis=0, tiled=True)]
    all_to_all x2 -> x0, local copies, waits for them, and re-layouts: 2.8 us -> none  [shards(): lax.all_to_all(grad_rows, 'blk', split_axis=1, concat_axis=0, tiled=True)]
  transfers between devices with their start and end apart: 4 -> 6, of which waited for: 3 -> 3; matrix products, arithmetic and copies ran while one was open for 7% -> 10% of each run, Pallas kernels for 0% -> 0%
where the time goes in v1:
time: 246 us
  waiting for transfers between devices  113 us (46%)
  blocking collectives  48.8 us (20%)
  matrix products  38.6 us (16%)
  local copies, waits for them, and re-layouts  22.9 us (9%)
  between operations  13.9 us (6%)
  other arithmetic  6.13 us (2%)
    all_gather x1, waiting for transfers between devices, shards(): everything = lax.all_gather(weighted, 'blk', axis=0, tiled=True)  80.9 us
    all_to_all x1, blocking collectives, shards(): lax.all_to_all(left_rows, 'expert', split_axis=0, concat_axis=1, tiled=True)  48.8 us
    dot_general x1, matrix products, shards(): jnp.dot(inverse_rows, everything, preferred_element_type=jnp.float32)  19.7 us
    ppermute x3, waiting for transfers between devices, shards(): part = lax.ppermute(part, 'blk', [(d, d ^ mask) for d in range(ways)])  16.7 us
    all_gather x1, waiting for transfers between devices, shards(): lax.all_gather(arrived, 'blk', axis=2, tiled=True)[0]  15.3 us
    dot_general x1, matrix products, shards(): jnp.dot(picked, lax.all_gather(arrived, 'blk', axis=2, tiled=True)[0], pr...  14.1 us
    gather x1, local copies, waits for them, and re-layouts, shards(): jnp.take(gradient, row_index, axis=1)  8.06 us
    broadcast_in_dim x1, local copies, waits for them, and re-layouts, shards(): return result[None]  6.56 us
  transfers between devices with their start and end apart: 6, of which 3 were waited for; matrix products, arithmetic and copies ran while one was open for 10% of the time, Pallas kernels for 0%

profile of v1, /device:TPU:0, one launch (start us, length us, event | category | flops | bytes accessed | tf_op | source)
XLA Modules:
  0.0 245.6 jit_solution(5899055387340232381)
XLA Ops:
  7.2 2.0 bitcast_select_fusion
  9.2 0.0 all-gather.6.cloned.1.call-start
  9.3 48.8 %all_to_all.12 = bf16[8,288,384]{2,1,0:T(8,128)(2,1)} all-to-all(bf16[8,288,384]{2,1,0:T(8,128)(2,1)} %param.9), channel_id=1, replica_groups=mesh['expert'=8,'blk'=4] {'expert'}, dimensions={0} | all-to-all | bytes 3538944 | tf_op jit(solution)/shard_map/all_to_all | solution.py:46
  58.1 0.0 all-gather.6.cloned.1.call-update
  58.1 0.0 all-gather.8.cloned.1.call-start
  58.2 0.1 dynamic-slice_bitcast_fusion
  58.3 0.1 collective-permute-start.2
  58.4 1.6 collective-permute-start
  60.0 0.5 collective-permute-start.1
  60.5 0.7 fusion.19
  61.2 0.2 reduce-window.8
  61.4 1.2 bitcast_subtract_fusion
  62.6 0.1 add_minimum_fusion
  62.7 0.7 min.26
  63.3 1.3 compare_and_fusion
  64.6 0.6 iota_compare_fusion
  65.3 0.7 min.28
  66.0 0.7 fusion.18
  66.7 0.7 lt.81
  67.4 1.3 broadcast_in_dim.43
  68.8 0.8 bitcast_dynamic-update-slice_fusion
  69.6 1.8 constant_dynamic-update-slice_fusion.2
  71.3 16.7 %collective-permute-done.1 = bf16[192,1024]{1,0:T(8,128)(2,1)S(1)} collective-permute-done((bf16[192,1024]{1,0:T(8,128)(2,1)S(1)}, bf16[192,1024]{1,0:T(8,128)(2,1)S(1)}, u32[]{:S(2)}, u32[]{:S(2)}) %collective-permute-start.1) | collective-permute-done | bytes 393248 | tf_op jit(solution)/shard_map/ppermute | solution.py:25
  88.1 0.8 constant_dynamic-update-slice_fusion.1
  88.8 0.8 constant_dynamic-update-slice_fusion
  89.6 4.8 %convolution_convert_fusion = bf16[1024,1536]{0,1:T(8,128)(2,1)S(1)} fusion(bf16[768,1024]{1,0:T(8,128)(2,1)} %constant_dynamic-update-slice_fusion, bf16[768,1536]{1,0:T(8,128)(2,1)} %all-gather.4.cloned.1.call-done), kind=kOutput, calls=%fused_computation.11 | convolution fusion | flops 2417491968 | bytes 7077888 | tf_op jit(solution)/shard_map/dot_general | solution.py:28
  94.4 8.1 %gather_fusion = bf16[2304,1024]{1,0:T(8,128)(2,1)} fusion(bf16[1024,1536]{0,1:T(8,128)(2,1)S(1)} %convolution_convert_fusion, s32[3072]{0:T(1024)S(1)} %pad_clamp_fusion), kind=kCustom, calls=%fused_computation | custom fusion | bytes 9446400 | tf_op jit(solution)/shard_map/jit(_take)/gather | solution.py:44
  102.5 15.3 %all-gather.6.cloned.1.call-done = bf16[1,2304,1536]{2,1,0:T(8,128)(2,1)} async-done(((bf16[1,2304,384]{2,1,0:T(8,128)(2,1)}), bf16[1,2304,1536]{2,1,0:T(8,128)(2,1)}) %all-gather.6.cloned.1.call-update) | async-done | bytes 7077904 | tf_op jit(solution)/shard_map/all_gather | solution.py:49
  117.8 14.1 %fusion.11 = bf16[1024,1536]{1,0:T(8,128)(2,1)} fusion(bf16[1,2304,1536]{2,1,0:T(8,128)(2,1)} %all-gather.6.cloned.1.call-done, bf16[2304,1024]{1,0:T(8,128)(2,1)} %gather_fusion, pred[2304]{0:T(1024)(128)(4,1)S(1)} %copy-done.1, pred[2304]{0:T(1024)(128)(4,1)S(1)} %copy-done.2), kind=kOutput, calls=%fused_computation.10 | convolution fusion | flops 7254048768 | bytes 14946816 | tf_op jit(solution)/shard_map/dot_general | solution.py:47
  132.0 80.9 %all-gather.8.cloned.1.call-done = bf16[4096,1536]{1,0:T(8,128)(2,1)} async-done(((bf16[1024,1536]{1,0:T(8,128)(2,1)}), bf16[4096,1536]{1,0:T(8,128)(2,1)}) %all-gather.8.cloned.1.call-update) | async-done | bytes 12582928 | tf_op jit(solution)/shard_map/all_gather | solution.py:53
  212.9 19.7 %fusion.8 = f32[1,1024,1536]{1,2,0:T(8,128)} fusion(bf16[4096,1536]{1,0:T(8,128)(2,1)} %all-gather.8.cloned.1.call-done, bf16[1,1024,4096]{2,1,0:T(8,128)(2,1)} %param.11), kind=kOutput, calls=%fused_computation.9 | convolution fusion | flops 12884901888 | bytes 27262976 | tf_op jit(solution)/shard_map/dot_general | solution.py:54
  232.5 6.6 %copy.7 = f32[1,1024,1536]{2,1,0:T(8,128)} copy(f32[1,1024,1536]{1,2,0:T(8,128)} %fusion.8) | data formatting | bytes 12582912 | tf_op jit(solution)/shard_map/broadcast_in_dim | solution.py:55
  (14 shorter events, 0.1 us)
Async XLA Ops:
  6.5 83.1 %all-gather.4.cloned.1.call-start = ((), (), s32[]{:S(2)}) async-start(), calls=%async_computation.1 | async-start | bytes 2949120 | tf_op jit(solution)/shard_map/all_gather | solution.py:30
  9.2 49.0 %copy-start = (bf16[1,192,4096]{2,1,0:T(8,128)(2,1)S(1)}, bf16[1,192,4096]{2,1,0:T(8,128)(2,1)}, u32[]{:S(2)}) copy-start(bf16[1,192,4096]{2,1,0:T(8,128)(2,1)} %param.7) | copy-start | bytes 4718596
  9.2 108.6 %all-gather.6.cloned.1.call-start = ((), (), s32[]{:S(2)}) async-start(), calls=%async_computation.2 | async-start | bytes 8847360 | tf_op jit(solution)/shard_map/all_gather | solution.py:49
  58.1 154.8 %all-gather.8.cloned.1.call-start = ((), (), s32[]{:S(2)}) async-start(), calls=%async_computation.3 | async-start | bytes 15728640 | tf_op jit(solution)/shard_map/all_gather | solution.py:53
  58.3 30.5 %collective-permute-start.2 = (bf16[192,1024]{1,0:T(8,128)(2,1)S(1)}, bf16[192,1024]{1,0:T(8,128)(2,1)S(1)}, u32[]{:S(2)}, u32[]{:S(2)}) collective-permute-start(bf16[192,1024]{1,0:T(8,128)(2,1)S(1)} %get-tuple-element.7), channel_id=1, source_target_pairs={{0,3},{1,2},{2,1},{3,0},{4,7},{5,6},{6,5},{7,4},{8,11},{9,10},{10,... | collective-permute-start | bytes 1179656 | tf_op jit(solution)/shard_map/ppermute | solution.py:25
  58.4 11.1 %collective-permute-start = (bf16[192,1024]{1,0:T(8,128)(2,1)S(1)}, bf16[192,1024]{1,0:T(8,128)(2,1)}, u32[]{:S(2)}, u32[]{:S(2)}) collective-permute-start(bf16[192,1024]{1,0:T(8,128)(2,1)S(1)} %get-tuple-element.8), channel_id=1, source_target_pairs={{0,1},{1,0},{2,3},{3,2},{4,5},{5,4},{6,7},{7,6},{8,9},{9,8},{10,11... | collective-permute-start | bytes 1179656 | tf_op jit(solution)/shard_map/ppermute | solution.py:25
  60.0 28.1 %collective-permute-start.1 = (bf16[192,1024]{1,0:T(8,128)(2,1)S(1)}, bf16[192,1024]{1,0:T(8,128)(2,1)S(1)}, u32[]{:S(2)}, u32[]{:S(2)}) collective-permute-start(bf16[192,1024]{1,0:T(8,128)(2,1)S(1)} %get-tuple-element.9), channel_id=1, source_target_pairs={{0,2},{1,3},{2,0},{3,1},{4,6},{5,7},{6,4},{7,5},{8,10},{9,11},{10,... | collective-permute-start | bytes 1179656 | tf_op jit(solution)/shard_map/ppermute | solution.py:25
  94.4 23.4 %copy-start.1 = (pred[2304]{0:T(1024)(128)(4,1)S(1)}, pred[2304]{0:T(1024)(128)(4,1)}, u32[]{:S(2)}) copy-start(pred[2304]{0:T(1024)(128)(4,1)} %lt.81) | copy-start | bytes 6916
  94.4 23.4 %copy-start.2 = (pred[2304]{0:T(1024)(128)(4,1)S(1)}, pred[2304]{0:T(1024)(128)(4,1)}, u32[]{:S(2)}) copy-start(pred[2304]{0:T(1024)(128)(4,1)} %compare_and_fusion) | copy-start | bytes 6916
Sparse Core Ops, SparseCore 0:
  9.3 26.7 all-gather.3
  58.2 59.4 all-gather.5
  132.1 80.7 all-gather.7
